TPU v7x, 256 devices: a whole 4x4x8 slice. The times are simulated.
256 devices in a mesh: seq: 64 (over x, z, core), head: 4 (over y).
Axes of the slice: x: 4, y: 4, z: 8, core: 2. Of those that a mesh axis runs over, the one named last changes fastest.
Arguments:
- frames: bfloat16 [16384, 1024], P('seq'), may hold values from -6 to 6
- norm_gain: float32 [1024], replicated, may hold values from 0.5 to 1.5
- w_qkv: bfloat16 [3, 1024, 1024], P(None, None, 'head'), may hold values from -2 to 2
- w_out: bfloat16 [1024, 1024], P('head'), may hold values from -0.1875 to 0.1875
- w_proj: bfloat16 [1024, 512], replicated, may hold values from -0.1875 to 0.1875
- text_table: bfloat16 [32768, 512], P(('seq', 'head')), may hold values from -6 to 6
- token_ids: int32 [512, 16], replicated, may hold values from 0 to 32767
- span_bounds: int32 [512, 2], P(('seq', 'head')), may hold values from 0 to 16384, as said below
- contrast_divisor: float32 [1], replicated, may hold values from 10 to 30
Outputs:
- interval_embedding_derivative: float32 [512, 512], P(('seq', 'head'))
- loss_terms: float32 [512], P(('seq', 'head'))
Inputs may be any that keep to these rules, and one draw needn't show every extreme that they name: `span_bounds`: both entries are multiples of 128 and the first is smaller than the second.
All inputs are finite; a program needn't handle non-finite values.
Results may differ from a plain program's by a relative error of at most 0.006.
Values may be sent and summed in bfloat16 or wider, within the bound.
A program may use at most 64 MiB of HBM per device.

v0:
```python
import jax
import jax.numpy as jnp
from jax import lax
from jax.sharding import PartitionSpec as P

HDIM = 64
E = 512
BLK = 128


def extended(cells, sides, width):
    for axis, dim in sides:
        count = lax.axis_size(axis)
        ends = count - 1
        head = lax.slice_in_dim(cells, 0, width, axis=dim)
        tail = lax.slice_in_dim(cells, cells.shape[dim] - width, cells.shape[dim], axis=dim)
        cells = jnp.concatenate(
            [
                lax.ppermute(tail, axis, [(i, (i + 1) % count) for i in range(ends)]),
                cells,
                lax.ppermute(head, axis, [((i + 1) % count, i) for i in range(ends)]),
            ],
            axis=dim,
        )
    return cells


def log_total(values, axis):
    return jnp.log(jnp.sum(jnp.exp(values), axis=axis))


def unit_rows(values):
    return (
        values * lax.rsqrt(jnp.mean(values * values, axis=-1, keepdims=True) + 1e-06) * E ** (-0.5)
    )


def token_counts(chosen, vocab_ids):

    def add_token(position, counts):
        column = lax.dynamic_index_in_dim(chosen, position, 1, keepdims=False)
        return counts + (column[:, None] == vocab_ids[None, :]).astype(jnp.float32)

    return lax.fori_loop(
        0, chosen.shape[1], add_token, jnp.zeros((chosen.shape[0], vocab_ids.shape[0]), jnp.float32)
    )


def local(
    frames, norm_gain, w_qkv, w_out, w_proj, text_table, token_ids, span_bounds, contrast_divisor
):
    frame_rows = frames.shape[0]
    head_cols = w_qkv.shape[2]
    local_heads = head_cols // HDIM
    seq_count = lax.axis_size("seq")
    total_frames = frame_rows * seq_count
    first_frame = lax.axis_index("seq") * frame_rows
    as32 = frames.astype(jnp.float32)
    normed = (
        as32 * lax.rsqrt(jnp.mean(as32 * as32, axis=-1, keepdims=True) + 1e-05) * norm_gain
    ).astype(jnp.bfloat16)
    queries = jnp.dot(normed, w_qkv[0], preferred_element_type=jnp.float32).astype(jnp.bfloat16)
    keys_now = jnp.dot(normed, w_qkv[1], preferred_element_type=jnp.float32).astype(jnp.bfloat16)
    values_now = jnp.dot(normed, w_qkv[2], preferred_element_type=jnp.float32).astype(jnp.bfloat16)
    pairs = jnp.concatenate([keys_now, values_now], axis=1)
    padded = extended(pairs, (("seq", 0),), frame_rows)
    query_block = min(512, frame_rows)
    span_width = 2 * frame_rows + query_block

    def attend(block):
        begin = block * query_block
        query_part = queries.reshape(query_block, local_heads, HDIM)
        key_part = padded[:, :head_cols].reshape(span_width, local_heads, HDIM)
        value_part = padded[:, head_cols:].reshape(span_width, local_heads, HDIM)
        scores = jnp.einsum(
            "qhd,khd->hqk", query_part, key_part, preferred_element_type=jnp.float32
        ) * HDIM ** (-0.5)
        query_pos = first_frame + begin + jnp.arange(query_block, dtype=jnp.int32)
        key_pos = first_frame + begin - frame_rows + jnp.arange(span_width, dtype=jnp.int32)
        allowed = (
            (jnp.abs(query_pos[:, None] - key_pos[None, :]) <= frame_rows)
            & (key_pos >= 0)[None, :]
            & (key_pos < total_frames)[None, :]
        )
        scores = jnp.where(allowed[None], scores, -1e30)
        top = jnp.max(scores, axis=2, keepdims=True)
        probs = jnp.exp(scores - top)
        denom = jnp.sum(probs, axis=2)
        mixed = jnp.einsum(
            "hqk,khd->qhd",
            probs.astype(jnp.bfloat16),
            value_part,
            preferred_element_type=jnp.float32,
        )
        return (mixed / denom.T[:, :, None]).astype(jnp.bfloat16).reshape(query_block, head_cols)

    attended = lax.map(attend, jnp.arange(frame_rows // query_block, dtype=jnp.int32)).reshape(
        frame_rows, head_cols
    )
    block_count = frame_rows // BLK
    out_sums = attended.astype(jnp.float32).reshape(block_count, BLK, head_cols).sum(axis=1)
    head_slot = lax.axis_index("head")
    own_features = lax.dynamic_slice_in_dim(as32, head_slot * head_cols, head_cols, 1)
    feature_sums = own_features.reshape(block_count, BLK, head_cols).sum(axis=1)
    proj_rows = lax.dynamic_slice_in_dim(w_proj, head_slot * head_cols, head_cols, 0)
    through_out = jnp.dot(out_sums, w_out.astype(jnp.float32), precision=lax.Precision.HIGHEST)
    partial_value = jnp.dot(
        through_out, w_proj.astype(jnp.float32), precision=lax.Precision.HIGHEST
    ) + jnp.dot(feature_sums, proj_rows.astype(jnp.float32), precision=lax.Precision.HIGHEST)
    everyone = lax.all_gather(partial_value, ("seq", "head"), axis=0, tiled=True)
    head_count = lax.axis_size("head")
    block_table = (
        everyone.reshape(seq_count, head_count, block_count, -1)
        .sum(axis=1)
        .reshape(seq_count * block_count, -1)
    )
    total_blocks = block_table.shape[0]
    block_ids = jnp.arange(total_blocks, dtype=jnp.int32)
    lower = span_bounds[:, 0] // BLK
    upper = span_bounds[:, 1] // BLK
    span_mask = (
        (block_ids[None, :] >= lower[:, None]) & (block_ids[None, :] < upper[:, None])
    ).astype(jnp.float32)
    pooled = jnp.dot(span_mask, block_table, precision=lax.Precision.HIGHEST)
    interval_embedding_rows = unit_rows(pooled).astype(jnp.bfloat16)
    own_caps = span_bounds.shape[0]
    all_caps = token_ids.shape[0]
    slot = lax.axis_index(("seq", "head"))
    first_caption = slot * own_caps
    vocab_rows = text_table.shape[0]
    vocab_ids = slot * vocab_rows + jnp.arange(vocab_rows, dtype=jnp.int32)
    counts = token_counts(token_ids, vocab_ids)
    raw = lax.psum_scatter(
        jnp.dot(counts.astype(jnp.bfloat16), text_table, preferred_element_type=jnp.float32),
        ("seq", "head"),
        scatter_dimension=0,
        tiled=True,
    )
    caption_own = unit_rows(raw).astype(jnp.bfloat16)
    spans_all, captions_all = (
        lax.all_gather(interval_embedding_rows, ("seq", "head"), axis=0, tiled=True),
        lax.all_gather(caption_own, ("seq", "head"), axis=0, tiled=True),
    )
    normalizer_divisor = contrast_divisor[0]
    row_logits = (
        jnp.einsum("je,ie->ji", caption_own, spans_all, preferred_element_type=jnp.float32)
        * normalizer_divisor
    )
    col_logits = (
        jnp.einsum(
            "je,ie->ji", captions_all, interval_embedding_rows, preferred_element_type=jnp.float32
        )
        * normalizer_divisor
    )
    row_total = log_total(row_logits, 1)
    col_total = log_total(col_logits, 0)
    own_square = lax.dynamic_slice_in_dim(row_logits, first_caption, own_caps, 1)
    loss_terms = 0.5 * (row_total + col_total) - jnp.diagonal(own_square)
    row_totals = lax.all_gather(row_total, ("seq", "head"), axis=0, tiled=True)
    marker = (
        jnp.arange(all_caps, dtype=jnp.int32)[:, None]
        == first_caption + jnp.arange(own_caps, dtype=jnp.int32)[None, :]
    ).astype(jnp.float32)
    derivative_multipliers = (
        0.5 * jnp.exp(col_logits - row_totals[:, None])
        + 0.5 * jnp.exp(col_logits - col_total[None, :])
        - marker
    ).astype(jnp.bfloat16)
    interval_embedding_derivative = (
        jnp.einsum(
            "ji,je->ie", derivative_multipliers, captions_all, preferred_element_type=jnp.float32
        )
        * normalizer_divisor
    )
    return (interval_embedding_derivative, loss_terms)


def solution(mesh):
    placed = (
        P("seq", None),
        P(),
        P(None, None, "head"),
        P("head", None),
        P(),
        P(("seq", "head"), None),
        P(),
        P(("seq", "head"), None),
        P(),
    )
    return jax.shard_map(
        local,
        mesh=mesh,
        in_specs=placed,
        out_specs=(P(("seq", "head"), None), P(("seq", "head"))),
        check_vma=False,
    )
```

profile of v0, /device:TPU:1, one launch (start us, length us, event | category | flops | bytes accessed | tf_op | source)
XLA Modules:
  0.0 622.0 jit_solution(1436011307544993010)
XLA Ops:
  7.2 1.3 multiply_reduce_fusion
  8.5 1.7 convolution_convert_fusion.1
  10.3 1.7 convolution_convert_fusion.2
  12.0 5.1 collective-permute-start
  17.0 2.2 collective-permute-start.1
  19.2 14.5 %while.18 = (s32[]{:T(128)}, f32[512,128]{1,0:T(8,128)S(1)}, s32[512,16]{0,1:T(8,128)}, s32[]{:T(128)}, s32[]{:T(128)}, /*index=5*/s32[]{:T(128)}) while((s32[]{:T(128)}, f32[512,128]{1,0:T(8,128)S(1)}, s32[512,16]{0,1:T(8,128)}, s32[]{:T(128)}, s32[]{:T(128)}, /*index=5*/s32[]{:T(128)}) %tuple.47), condition=%wide.region_1.2_spmd.clone, body=%wide.region_0.0_spmd.clone.sunk | while | flops 262275 | bytes 531543 | solution.py:44
  19.2 0.7 constant_dynamic-slice_fusion.4
  20.2 0.7 constant_dynamic-slice_fusion.4
  21.1 0.7 constant_dynamic-slice_fusion.4
  22.0 0.7 constant_dynamic-slice_fusion.4
  22.9 0.7 constant_dynamic-slice_fusion.4
  23.8 0.7 constant_dynamic-slice_fusion.4
  24.7 0.7 constant_dynamic-slice_fusion.4
  25.6 0.7 constant_dynamic-slice_fusion.4
  26.5 0.7 constant_dynamic-slice_fusion.4
  27.4 0.7 constant_dynamic-slice_fusion.4
  28.3 0.7 constant_dynamic-slice_fusion.4
  29.2 0.7 constant_dynamic-slice_fusion.4
  30.1 0.7 constant_dynamic-slice_fusion.4
  31.0 0.7 constant_dynamic-slice_fusion.4
  31.9 0.7 constant_dynamic-slice_fusion.4
  32.8 0.7 constant_dynamic-slice_fusion.4
  33.7 1.3 fusion.30
  35.2 0.3 fusion.22
  35.7 1.5 convolution_convert_fusion
  37.2 1.1 pad_maximum_fusion
  38.4 0.8 fusion.2
  39.2 0.9 fusion.3
  40.1 1.0 fusion.18
  41.3 0.3 reduce_sum.85
  41.7 0.4 fusion.56
  42.0 0.5 fusion.57
  42.5 0.8 fusion.11
  44.4 251.9 %all-reduce.4.cloned.1.call-done = f32[512,512]{1,0:T(8,128)} async-done(((f32[512,512]{1,0:T(8,128)}), f32[512,512]{1,0:T(8,128)}) %all-reduce.4.cloned.1.call-update) | async-done | bytes 1048592
  296.3 0.8 multiply_reduce_fusion.2
  297.1 0.8 fusion.74
  297.9 118.1 %all-gather = bf16[256,2,512]{2,1,0:T(2,128)(2,1)S(1)} all-gather(bf16[1,2,512]{2,1,0:T(2,128)(2,1)S(1)} %fusion.74), channel_id=1, replica_groups=mesh['seq'=64,'head'=4] {'seq','head'}, dimensions={0}, use_global_device_ids=true | all-gather | bytes 526336 | tf_op jit(solution)/shard_map/all_gather | solution.py:142
  416.1 0.2 reshape.160
  416.3 1.8 bitcast_reduce_fusion
  418.3 0.3 multiply_reduce_fusion.1
  418.7 116.9 %all-gather.2 = bf16[256,2,512]{2,1,0:T(2,128)(2,1)S(1)} all-gather(bf16[1,2,512]{2,1,0:T(2,128)(2,1)S(1)} %fusion.73), channel_id=1, replica_groups=mesh['seq'=64,'head'=4] {'seq','head'}, dimensions={0}, use_global_device_ids=true | all-gather | bytes 526336 | tf_op jit(solution)/shard_map/all_gather | solution.py:141
  535.6 0.2 reshape.164
  535.8 1.1 exponential_reduce_fusion.1
  536.9 0.6 gather_fusion
  537.6 0.4 exponential_reduce_fusion
  537.9 0.5 multiply_subtract_fusion
  538.5 75.9 %all-reduce = f32[512]{0:T(512)S(1)} all-reduce(f32[512]{0:T(512)S(1)} %get-tuple-element.129), channel_id=1, replica_groups=mesh['seq'=64,'head'=4] {'seq','head'}, use_global_device_ids=true, to_apply=%add | all-reduce | flops 512 | bytes 4096
  614.4 0.8 convolution_multiply_fusion
  (70 shorter events, 3.7 us)
Async XLA Ops:
  7.2 34.9 %copy-start = (bf16[1024,512]{1,0:T(8,128)(2,1)S(1)}, bf16[1024,512]{1,0:T(8,128)(2,1)}, u32[]{:S(2)}) copy-start(bf16[1024,512]{1,0:T(8,128)(2,1)} %param.15) | copy-start | bytes 3145732
  7.2 289.1 %all-reduce.4.cloned.1.call-start = ((), (), s32[]{:S(2)}) async-start(), calls=%async_computation.1 | async-start | bytes 2097152
  8.5 25.2 %copy-start.3 = (bf16[128,512]{1,0:T(8,128)(2,1)S(1)}, bf16[128,512]{1,0:T(8,128)(2,1)}, u32[]{:S(2)}) copy-start(bf16[128,512]{1,0:T(8,128)(2,1)} %param.16) | copy-start | bytes 393220
  11.9 23.6 %copy-start.1 = (bf16[256,1024]{1,0:T(8,128)(2,1)S(1)}, bf16[256,1024]{1,0:T(8,128)(2,1)}, u32[]{:S(2)}) copy-start(bf16[256,1024]{1,0:T(8,128)(2,1)} %param.11) | copy-start | bytes 1572868
  12.0 25.2 %collective-permute-start = (bf16[256,512]{0,1:T(8,128)(2,1)S(1)}, bf16[256,512]{0,1:T(8,128)(2,1)}, u32[]{:S(2)}, u32[]{:S(2)}) collective-permute-start(bf16[256,512]{0,1:T(8,128)(2,1)S(1)} %pad_maximum_fusion.1), channel_id=1, source_target_pairs={{0,4},{4,8},{8,12},{12,16},{16,20},{20,24},{24,28},{28,32},{32,36}... | collective-permute-start | bytes 786440 | tf_op jit(solution)/shard_map/ppermute | solution.py:19
  17.0 20.2 %collective-permute-start.1 = (bf16[256,512]{0,1:T(8,128)(2,1)S(1)}, bf16[256,512]{0,1:T(8,128)(2,1)}, u32[]{:S(2)}, u32[]{:S(2)}) collective-permute-start(bf16[256,512]{0,1:T(8,128)(2,1)S(1)} %pad_maximum_fusion.1), channel_id=1, source_target_pairs={{4,0},{8,4},{12,8},{16,12},{20,16},{24,20},{28,24},{32,28},{36,32}... | collective-permute-start | bytes 786440 | tf_op jit(solution)/shard_map/ppermute | solution.py:21
  19.2 16.5 %copy-start.5 = (f32[1024]{0:T(1024)S(1)}, f32[1024]{0:T(1024)}, u32[]{:S(2)}) copy-start(f32[1024]{0:T(1024)} %param.12) | copy-start | bytes 12292
  35.1 381.2 %all-gather.5.cloned.1.call-start = ((), (), s32[]{:S(2)}) async-start(), calls=%async_computation | async-start | bytes 1052672 | tf_op jit(solution)/shard_map/all_gather | solution.py:110
  40.1 1.6 copy-start.2
  40.1 4.1 copy-start.4
Sparse Core Ops, SparseCore 0:
  35.2 261.0 all-reduce.3
  300.6 103.6 all-gather.4
where the time goes:
time: 624 us; the launch traced here: 622 us
  blocking collectives  311 us (50%)
  waiting for transfers between devices  252 us (40%)
  between operations  15 us (2%)
  local copies, waits for them, and re-layouts  13.2 us (2%)
  matrix products  12.3 us (2%)
  other arithmetic  11 us (2%)
  starting transfers between devices  7.3 us (1%)
    unnamed x3, waiting for transfers between devices  252 us
    all_gather x1, blocking collectives, local(): lax.all_gather(caption_own, ('seq', 'head'), axis=0, tiled=True)  118 us
    all_gather x1, blocking collectives, local(): lax.all_gather(interval_embedding_rows, ('seq', 'head'), axis=0, tiled=True)  117 us
    unnamed x1, blocking collectives  75.9 us
  transfers between devices with their start and end apart: 4, of which 1 were waited for; matrix products, arithmetic and copies ran while one was open for 4% of the time, Pallas kernels for 0%

commit v1 on v0

--- a/solution.py
+++ b/solution.py
@@ -6,6 +6,11 @@
 HDIM = 64
 E = 512
 BLK = 128
+
+
+def swapped_in(block, axis, dim):
+    sent = jnp.stack([block] * lax.axis_size(axis))
+    return jnp.concatenate(lax.all_to_all(sent, axis, 0, 0), axis=dim)
 
 
 def extended(cells, sides, width):
@@ -138,7 +143,7 @@
     )
     caption_own = unit_rows(raw).astype(jnp.bfloat16)
     spans_all, captions_all = (
-        lax.all_gather(interval_embedding_rows, ("seq", "head"), axis=0, tiled=True),
+        swapped_in(interval_embedding_rows, ("seq", "head"), 0),
         lax.all_gather(caption_own, ("seq", "head"), axis=0, tiled=True),
     )
     normalizer_divisor = contrast_divisor[0]

time: 624 us -> 608 us (0.974)
  blocking collectives: 311 us -> 194 us
  waiting for transfers between devices: 252 us -> 342 us
  starting transfers between devices: 7.3 us -> 17.7 us
    all_gather x1 -> x0, blocking collectives: 117 us -> none  [local(): lax.all_gather(interval_embedding_rows, ('seq', 'head'), axis=0, tiled=True)]
    all_gather x1, waiting for transfers between devices: 0.02 us -> 88.9 us  [local(): lax.all_gather(partial_value, ('seq', 'head'), axis=0, tiled=True)]
    all_to_all x0 -> x1, starting transfers between devices: none -> 10.5 us  [swapped_in(): return jnp.concatenate(lax.all_to_all(sent, axis, 0, 0), axis=dim)]
  transfers between devices with their start and end apart: 4 -> 5, of which waited for: 1 -> 3; matrix products, arithmetic and copies ran while one was open for 4% -> 4% of each run, Pallas kernels for 0% -> 0%
where the time goes in v1:
time: 608 us; the launch traced here: 606 us
  waiting for transfers between devices  342 us (56%)
  blocking collectives  194 us (32%)
  starting transfers between devices  17.7 us (3%)
  between operations  15 us (2%)
  local copies, waits for them, and re-layouts  14.2 us (2%)
  matrix products  12.2 us (2%)
  other arithmetic  11.7 us (2%)
    unnamed x3, waiting for transfers between devices  249 us
    all_gather x1, blocking collectives, local(): lax.all_gather(caption_own, ('seq', 'head'), axis=0, tiled=True)  118 us
    all_gather x1, waiting for transfers between devices, local(): lax.all_gather(partial_value, ('seq', 'head'), axis=0, tiled=True)  88.9 us
    unnamed x1, blocking collectives  75.6 us
  transfers between devices with their start and end apart: 5, of which 3 were waited for; matrix products, arithmetic and copies ran while one was open for 4% of the time, Pallas kernels for 0%

profile of v1, /device:TPU:1, one launch (start us, length us, event | category | flops | bytes accessed | tf_op | source)
XLA Modules:
  0.0 606.4 jit_solution(1245762500219217627)
XLA Ops:
  7.2 1.3 multiply_reduce_fusion
  8.6 1.7 convolution_convert_fusion.1
  10.3 1.7 convolution_convert_fusion.2
  11.9 0.7 pad_maximum_fusion.1
  12.7 4.9 collective-permute-start
  17.6 2.2 collective-permute-start.1
  20.3 1.5 convolution_convert_fusion
  21.8 3.8 collective-permute-done.1
  25.6 1.1 pad_maximum_fusion
  26.7 0.8 fusion.2
  27.5 0.9 fusion.3
  28.5 1.0 fusion.18
  29.7 0.3 reduce_sum.85
  30.0 0.4 fusion.56
  30.4 0.5 fusion.57
  30.9 0.8 fusion.11
  31.8 14.5 %while.18 = (s32[]{:T(128)}, f32[512,128]{1,0:T(8,128)S(1)}, s32[512,16]{0,1:T(8,128)}, s32[]{:T(128)}, s32[]{:T(128)}, /*index=5*/s32[]{:T(128)}) while((s32[]{:T(128)}, f32[512,128]{1,0:T(8,128)S(1)}, s32[512,16]{0,1:T(8,128)}, s32[]{:T(128)}, s32[]{:T(128)}, /*index=5*/s32[]{:T(128)}) %tuple.47), condition=%wide.region_1.2_spmd.clone, body=%wide.region_0.0_spmd.clone.sunk | while | flops 262275 | bytes 531543 | solution.py:49
  31.8 0.7 constant_dynamic-slice_fusion.4
  32.7 0.7 constant_dynamic-slice_fusion.4
  33.6 0.7 constant_dynamic-slice_fusion.4
  34.5 0.7 constant_dynamic-slice_fusion.4
  35.4 0.7 constant_dynamic-slice_fusion.4
  36.3 0.7 constant_dynamic-slice_fusion.4
  37.2 0.7 constant_dynamic-slice_fusion.4
  38.2 0.7 constant_dynamic-slice_fusion.4
  39.1 0.7 constant_dynamic-slice_fusion.4
  40.0 0.7 constant_dynamic-slice_fusion.4
  40.9 0.7 constant_dynamic-slice_fusion.4
  41.8 0.7 constant_dynamic-slice_fusion.4
  42.7 0.7 constant_dynamic-slice_fusion.4
  43.6 0.7 constant_dynamic-slice_fusion.4
  44.5 0.7 constant_dynamic-slice_fusion.4
  45.4 0.7 constant_dynamic-slice_fusion.4
  46.3 1.3 fusion.30
  48.6 88.9 %all-gather.4.cloned.1.call-done = f32[256,2,512]{2,1,0:T(2,128)} async-done(((f32[1,2,512]{2,1,0:T(2,128)}), f32[256,2,512]{2,1,0:T(2,128)}) %all-gather.4.cloned.1.call-update) | async-done | bytes 1048592 | tf_op jit(solution)/shard_map/all_gather | solution.py:115
  137.5 1.8 bitcast_reduce_fusion
  139.9 1.1 stack.2
  141.0 10.5 %all-to-all-start = ((bf16[256,2,512]{2,1,0:T(2,128)(2,1)}), bf16[256,2,512]{2,1,0:T(2,128)(2,1)S(1)}, u32[]{:S(2)}, u32[]{:S(2)}) async-start(bf16[256,2,512]{2,1,0:T(2,128)(2,1)} %stack.2), calls=%async_computation | async-start | bytes 1048576 | tf_op jit(solution)/shard_map/all_to_all | solution.py:13
  151.6 248.9 %all-reduce.4.cloned.1.call-done = f32[512,512]{1,0:T(8,128)} async-done(((f32[512,512]{1,0:T(8,128)}), f32[512,512]{1,0:T(8,128)}) %all-reduce.4.cloned.1.call-update) | async-done | bytes 1048592
  400.4 0.8 multiply_reduce_fusion.2
  401.3 0.8 fusion.73
  402.1 118.0 %all-gather = bf16[256,2,512]{2,1,0:T(2,128)(2,1)S(1)} all-gather(bf16[1,2,512]{2,1,0:T(2,128)(2,1)S(1)} %fusion.73), channel_id=1, replica_groups=mesh['seq'=64,'head'=4] {'seq','head'}, dimensions={0}, use_global_device_ids=true | all-gather | bytes 526336 | tf_op jit(solution)/shard_map/all_gather | solution.py:147
  520.3 0.4 exponential_reduce_fusion
  520.8 1.1 exponential_reduce_fusion.1
  522.0 0.6 gather_fusion
  522.7 0.5 multiply_subtract_fusion
  523.2 75.6 %all-reduce = f32[512]{0:T(512)S(1)} all-reduce(f32[512]{0:T(512)S(1)} %get-tuple-element.129), channel_id=1, replica_groups=mesh['seq'=64,'head'=4] {'seq','head'}, use_global_device_ids=true, to_apply=%add | all-reduce | flops 512 | bytes 4096
  598.8 0.8 convolution_multiply_fusion
  (72 shorter events, 4.7 us)
Async XLA Ops:
  7.2 23.2 %copy-start = (bf16[1024,512]{1,0:T(8,128)(2,1)S(1)}, bf16[1024,512]{1,0:T(8,128)(2,1)}, u32[]{:S(2)}) copy-start(bf16[1024,512]{1,0:T(8,128)(2,1)} %param.15) | copy-start | bytes 3145732
  7.2 12.9 %copy-start.1 = (bf16[256,1024]{1,0:T(8,128)(2,1)S(1)}, bf16[256,1024]{1,0:T(8,128)(2,1)}, u32[]{:S(2)}) copy-start(bf16[256,1024]{1,0:T(8,128)(2,1)} %param.11) | copy-start | bytes 1572868
  7.2 130.4 %all-gather.4.cloned.1.call-start = ((), (), s32[]{:S(2)}) async-start(), calls=%async_computation.1 | async-start | bytes 1052672 | tf_op jit(solution)/shard_map/all_gather | solution.py:115
  8.6 11.7 %copy-start.5 = (f32[1024]{0:T(1024)S(1)}, f32[1024]{0:T(1024)}, u32[]{:S(2)}) copy-start(f32[1024]{0:T(1024)} %param.12) | copy-start | bytes 12292
  12.7 9.2 %collective-permute-start = (bf16[256,512]{0,1:T(8,128)(2,1)}, bf16[256,512]{0,1:T(8,128)(2,1)}, u32[]{:S(2)}, u32[]{:S(2)}) collective-permute-start(bf16[256,512]{0,1:T(8,128)(2,1)} %pad_maximum_fusion.1), channel_id=1, source_target_pairs={{0,4},{4,8},{8,12},{12,16},{16,20},{20,24},{24,28},{28,32},{32,36}... | collective-permute-start | bytes 786440 | tf_op jit(solution)/shard_map/ppermute | solution.py:24
  17.6 8.0 %collective-permute-start.1 = (bf16[256,512]{0,1:T(8,128)(2,1)}, bf16[256,512]{0,1:T(8,128)(2,1)}, u32[]{:S(2)}, u32[]{:S(2)}) collective-permute-start(bf16[256,512]{0,1:T(8,128)(2,1)} %pad_maximum_fusion.1), channel_id=1, source_target_pairs={{4,0},{8,4},{12,8},{16,12},{20,16},{24,20},{28,24},{32,28},{36,32}... | collective-permute-start | bytes 786440 | tf_op jit(solution)/shard_map/ppermute | solution.py:26
  28.5 1.5 copy-start.2
  29.5 16.8 %copy-start.3 = (bf16[128,512]{1,0:T(8,128)(2,1)S(1)}, bf16[128,512]{1,0:T(8,128)(2,1)}, u32[]{:S(2)}) copy-start(bf16[128,512]{1,0:T(8,128)(2,1)} %param.16) | copy-start | bytes 393220
  30.4 17.4 %copy-start.4 = (s32[2,2]{1,0:T(2,128)S(1)}, s32[2,2]{1,0:T(2,128)}, u32[]{:S(2)}) copy-start(s32[2,2]{1,0:T(2,128)} %param.18) | copy-start | bytes 52
  31.7 368.7 %all-reduce.4.cloned.1.call-start = ((), (), s32[]{:S(2)}) async-start(), calls=%async_computation.2 | async-start | bytes 2097152
  141.0 379.6 %all-to-all-start = ((bf16[256,2,512]{2,1,0:T(2,128)(2,1)}), bf16[256,2,512]{2,1,0:T(2,128)(2,1)S(1)}, u32[]{:S(2)}, u32[]{:S(2)}) async-start(bf16[256,2,512]{2,1,0:T(2,128)(2,1)} %stack.2), calls=%async_computation | async-start | bytes 1048576 | tf_op jit(solution)/shard_map/all_to_all | solution.py:13
Sparse Core Ops, SparseCore 0:
  31.9 105.6 all-gather.3
  143.0 257.4 all-reduce.3
